TPU v7x, 128 devices: a whole 4x4x4 slice. The times are simulated.
128 devices in a mesh: section: 2 (over x_hi), seq: 16 (over z, y), mp: 4 (over x_lo, core).
Axes of the slice: x: 4 (x_hi: 2, x_lo: 2; x = x_hi * 2 + x_lo), y: 4, z: 4, core: 2. Of those that a mesh axis runs over, the one named last changes fastest.
Arguments:
- video: bfloat16 [2, 4, 128, 3072], P(None, None, 'seq'), may hold values from -6 to 6
- text: bfloat16 [2, 128, 3072], P(None, 'seq'), may hold values from -6 to 6
- patch_lengths: int32 [2, 4], replicated, may hold values from 1 to 128, 384 in all within a row
- text_len: int32 [2], replicated, may hold values from 64 to 128, as said below
- timestep: int32 [1], replicated, may hold values from 0 to 999
- w_mod: bfloat16 [2, 512, 9216], P('section', None, 'mp'), may hold values from -0.25 to 0.25
- w_qkv: bfloat16 [2, 3072, 3, 3072], P('section', None, None, 'mp')
- w_out: bfloat16 [2, 3072, 3072], P('section', 'mp'), may hold values from -0.109375 to 0.109375
- stale_cache: bfloat16 [2, 2, 4, 128, 2, 3072], P('section', None, None, 'seq', None, 'mp'), may hold values from -6 to 6
Outputs:
- hidden_video: bfloat16 [2, 2, 4, 128, 3072], P('section', None, None, 'seq')
- hidden_text: bfloat16 [2, 2, 128, 3072], P('section', None, 'seq')
- cache_video: bfloat16 [2, 2, 4, 128, 2, 3072], P('section', None, None, 'seq', None, 'mp')
- cache_text: bfloat16 [2, 2, 128, 2, 3072], P('section', None, 'seq', None, 'mp')
Inputs may be any that keep to these rules, and one draw needn't show every extreme that they name: `patch_lengths`: 4 patch lengths per request summing to 384; in every request the largest is 128. `text_len`: exactly one request has 128, every other fewer.
All inputs are finite; a program needn't handle non-finite values.
Results may differ from a plain program's by a relative error of at most 0.01.
Values may be sent and summed in bfloat16 or wider, within the bound.
No kernel may reach another device: no remote copies, remote signals or barrier semaphores. Data moves between devices by JAX's collectives and lax.ppermute only.
A program may use at most 192 MiB of HBM per device.

v0:
```python
import math
import jax
import jax.numpy as jnp
from jax import lax
from jax.sharding import PartitionSpec as P

HEAD = 64
EPS = 1e-05
NEG = -1e30


def passed_along(value, axis, steps):
    count = lax.axis_size(axis)
    leading, last = (max(0, -steps), min(count, count - steps))
    return lax.ppermute(value, axis, [(source, source + steps) for source in range(leading, last)])


def modulation(timestep, weight):
    half_width = weight.shape[0] // 2
    frequency = jnp.exp(-math.log(10000.0) * jnp.arange(half_width, dtype=jnp.float32) / half_width)
    phases = timestep.astype(jnp.float32)[0] * frequency
    embedding = jnp.concatenate([jnp.cos(phases), jnp.sin(phases)])
    active = jax.nn.silu(embedding).astype(jnp.bfloat16)
    return jnp.dot(active[None, :], weight, preferred_element_type=jnp.float32)[0]


def normalize(token_rows, shift_vec, scale_vec):
    values = token_rows.astype(jnp.float32)
    center = values - jnp.mean(values, axis=-1, keepdims=True)
    spread = jnp.mean(center * center, axis=-1, keepdims=True)
    return (center * lax.rsqrt(spread + EPS) * (1.0 + scale_vec) + shift_vec).astype(jnp.bfloat16)


def scores_of(query_heads, key_value, head_count):
    requests, key_count = (key_value.shape[0], key_value.shape[1])
    key_heads = key_value[:, :, 0].reshape(requests, key_count, head_count, HEAD)
    value_heads = key_value[:, :, 1].reshape(requests, key_count, head_count, HEAD)
    scores = jnp.einsum(
        "rqhe,rkhe->rhqk", query_heads, key_heads, preferred_element_type=jnp.float32
    ) * HEAD ** (-0.5)
    return (scores, value_heads)


def masked_max(scores, key_mask):
    return jnp.max(jnp.where(key_mask[:, None, None, :], scores, NEG), axis=-1)


def weighed(scores, key_mask, top_score, value_heads):
    weights = jnp.where(key_mask[:, None, None, :], jnp.exp(scores - top_score[..., None]), 0.0)
    weight_sum = jnp.sum(weights, axis=-1)
    accumulated = jnp.einsum(
        "rhqk,rkhe->rhqe",
        weights.astype(jnp.bfloat16),
        value_heads,
        preferred_element_type=jnp.float32,
    )
    return (weight_sum, accumulated)


def body(video, text, patch_lengths, text_len, timestep, w_mod, w_qkv, w_out, stale_cache):
    section_index = lax.axis_index("section")
    seq_count = lax.axis_size("seq")
    requests, patches, per_dev, model_width = video.shape
    text_dev = text.shape[1]
    capacity = per_dev * seq_count
    text_slots = text_dev * seq_count
    column_count = w_out.shape[1]
    head_count = column_count // HEAD
    row_count = per_dev + text_dev
    modulated = lax.all_gather(modulation(timestep, w_mod[0]), "mp", axis=0, tiled=True)
    shift_vec = modulated[:model_width]
    scale_vec = modulated[model_width : 2 * model_width]
    gate_vec = modulated[2 * model_width :]
    weight_qkv = w_qkv[0].reshape(model_width, 3 * column_count)
    weight_out = w_out[0]
    stale_local = stale_cache[0]
    slot_index = jnp.arange(capacity, dtype=jnp.int32)
    video_valid = (slot_index[None, None, :] < patch_lengths[:, :, None]).reshape(requests, -1)
    text_valid = jnp.arange(text_slots, dtype=jnp.int32)[None, :] < text_len[:, None]
    all_valid = jnp.concatenate([video_valid, text_valid], axis=1)
    video_patch = jnp.repeat(jnp.arange(patches, dtype=jnp.int32), capacity)
    all_patch = jnp.concatenate([video_patch, jnp.zeros((text_slots,), jnp.int32)])
    stale_whole = lax.all_gather(stale_local, "seq", axis=2, tiled=True).reshape(
        requests, patches * capacity, 2, column_count
    )
    fresh_video = jnp.zeros((requests, patches, capacity, 2, column_count), jnp.bfloat16)
    fresh_text = jnp.zeros((requests, text_slots, 2, column_count), jnp.bfloat16)
    own_video = jnp.zeros((requests, patches, per_dev, 2, column_count), jnp.bfloat16)
    own_text = jnp.zeros((requests, text_dev, 2, column_count), jnp.bfloat16)
    out_video = jnp.zeros((requests, patches, per_dev, model_width), jnp.bfloat16)
    out_text = jnp.zeros((requests, text_dev, model_width), jnp.bfloat16)
    received = jnp.zeros((requests, row_count, model_width), jnp.bfloat16)
    patch_ids = jnp.arange(patches, dtype=jnp.int32)
    for turn_index in range(patches + 1):
        patch_now = turn_index - section_index
        picked = lax.dynamic_index_in_dim(
            video, jnp.clip(patch_now, 0, patches - 1), 1, keepdims=False
        )
        token_rows = jnp.where(
            section_index == 0, jnp.concatenate([picked, text], axis=1), received
        )
        normed = normalize(token_rows, shift_vec, scale_vec)
        projected = jnp.dot(
            normed.reshape(-1, model_width), weight_qkv, preferred_element_type=jnp.float32
        )
        projected = projected.reshape(requests, row_count, 3, column_count).astype(jnp.bfloat16)
        queries = projected[:, :, 0]
        key_value = projected[:, :, 1:]
        gathered_video, gathered_text = (
            lax.all_gather(key_value[:, :per_dev], "seq", axis=1, tiled=True),
            lax.all_gather(key_value[:, per_dev:], "seq", axis=1, tiled=True),
        )
        current = patch_ids == patch_now
        fresh_video = jnp.where(
            current[None, :, None, None, None], gathered_video[:, None], fresh_video
        )
        fresh_text = jnp.where(patch_now == 0, gathered_text, fresh_text)
        own_video = jnp.where(
            current[None, :, None, None, None], key_value[:, None, :per_dev], own_video
        )
        own_text = jnp.where(patch_now == 0, key_value[:, per_dev:], own_text)
        fresh_all = jnp.concatenate(
            [fresh_video.reshape(requests, patches * capacity, 2, column_count), fresh_text], axis=1
        )
        fresh_mask = all_valid & (all_patch[None, :] <= patch_now)
        query_heads = queries.reshape(requests, row_count, head_count, HEAD)
        scores, value_heads = scores_of(query_heads, fresh_all, head_count)
        fresh_top = masked_max(scores, fresh_mask)
        fresh_sum, fresh_acc = weighed(scores, fresh_mask, fresh_top, value_heads)
        stale_mask = video_valid & (video_patch[None, :] > patch_now)
        scores, value_heads = scores_of(query_heads, stale_whole, head_count)
        stale_top = masked_max(scores, stale_mask)
        stale_sum, stale_acc = weighed(scores, stale_mask, stale_top, value_heads)
        top_score = jnp.maximum(fresh_top, stale_top)
        fresh_weight = jnp.exp(fresh_top - top_score)
        stale_weight = jnp.exp(stale_top - top_score)
        numer = fresh_acc * fresh_weight[..., None] + stale_acc * stale_weight[..., None]
        denom = fresh_sum * fresh_weight + stale_sum * stale_weight
        attended = (numer / denom[..., None]).astype(jnp.bfloat16)
        attended = attended.transpose(0, 2, 1, 3).reshape(requests * row_count, column_count)
        partial_out = jnp.dot(attended, weight_out, preferred_element_type=jnp.float32).reshape(
            requests, row_count, model_width
        )
        summed = lax.psum(partial_out, "mp")
        result = (token_rows.astype(jnp.float32) + gate_vec * summed).astype(jnp.bfloat16)
        out_video = jnp.where(current[None, :, None, None], result[:, None, :per_dev], out_video)
        out_text = jnp.where(patch_now == 0, result[:, per_dev:], out_text)
        if turn_index < patches:
            received = passed_along(result, "section", 1)
    return (out_video[None], out_text[None], own_video[None], own_text[None])


def solution(mesh):
    placed = (
        P(None, None, "seq", None),
        P(None, "seq", None),
        P(),
        P(),
        P(),
        P("section", None, "mp"),
        P("section", None, None, "mp"),
        P("section", "mp", None),
        P("section", None, None, "seq", None, "mp"),
    )
    return jax.shard_map(
        body,
        mesh=mesh,
        in_specs=placed,
        out_specs=(
            P("section", None, None, "seq", None),
            P("section", None, "seq", None),
            P("section", None, None, "seq", None, "mp"),
            P("section", None, "seq", None, "mp"),
        ),
        check_vma=False,
    )
```

profile of v0, /device:TPU:1, one launch (start us, length us, event | category | flops | bytes accessed | tf_op | source)
XLA Modules:
  0.0 716.3 jit_solution(2597853420989053191)
XLA Ops:
  8.0 18.7 %copy.75 = bf16[1,3072,3,768]{1,3,2,0:T(8,128)(2,1)} copy(bf16[1,3072,3,768]{3,1,2,0:T(8,128)(2,1)} %param.15) | data formatting | bytes 28311552 | tf_op args[6]
  27.8 6.4 all-gather.1
  35.4 9.3 %fusion.26 = bf16[2,16,3,768]{3,1,2,0:T(8,128)(2,1)S(1)} fusion(bf16[1,3072,3,768]{1,3,2,0:T(8,128)(2,1)} %copy.75, f32[3072]{0:T(1024)S(1)} %get-tuple-element.76, f32[3072]{0:T(1024)S(1)} %get-tuple-element.77, f32[2,16]{1,0:T(2,128)S(1)} %add_rsqrt_fusion.4, f32[2,16]{1,0:T(2,128)S(1)} %broadcast_multiply_fusion.4, ...), kind=kOutput, calls=%fused_computation.57 | convolution fusion | flops 454139904 | bytes 14524673 | tf_op jit(solution)/shard_map/dot_general | solution.py:103
  44.9 24.0 %all_gather.38 = bf16[2,128,2,768]{3,1,2,0:T(8,128)(2,1)S(1)} all-gather(bf16[2,8,2,768]{3,1,2,0:T(8,128)(2,1)S(1)} %get-tuple-element.73), channel_id=1, replica_groups=mesh['section'=2,'seq'=16,'mp'=4] {'seq'}, dimensions={1}, use_global_device_ids=true | all-gather | bytes 835584 | tf_op jit(solution)/shard_map/all_gather | solution.py:111
  70.1 17.7 %all_gather.37 = bf16[2,128,2,768]{3,1,2,0:T(8,128)(2,1)S(1)} all-gather(bf16[2,8,2,768]{3,1,2,0:T(8,128)(2,1)S(1)} %get-tuple-element.74), channel_id=1, replica_groups=mesh['section'=2,'seq'=16,'mp'=4] {'seq'}, dimensions={1}, use_global_device_ids=true | all-gather | bytes 835584 | tf_op jit(solution)/shard_map/all_gather | solution.py:110
  90.6 5.7 broadcast_in_dim.475
  102.9 9.3 %fusion.259 = (bf16[2,512,1,768]{3,2,1,0:T(2,128)(2,1)}, bf16[2,512,1,768]{3,2,1,0:T(2,128)(2,1)}) fusion(bf16[2,512,2,768]{3,2,1,0:T(2,128)(2,1)} %bitcast.353), kind=kLoop, calls=%fused_computation.383 | loop fusion | bytes 6291456 | tf_op jit(solution)/shard_map/slice | solution.py:36
  112.2 6.8 copy.115
  119.0 8.1 %copy.114 = bf16[2,512,1,768]{1,3,0,2:T(8,128)(2,1)} copy(bf16[2,512,1,768]{3,2,1,0:T(2,128)(2,1)} %get-tuple-element.51) | data formatting | bytes 3145728
  135.2 45.4 %all-reduce.7.cloned.1.call-done = f32[2,16,3072]{2,1,0:T(8,128)} async-done(((f32[2,16,3072]{2,1,0:T(8,128)}), f32[2,16,3072]{2,1,0:T(8,128)}) %all-reduce.7.cloned.1.call-update) | async-done | bytes 393232 | tf_op jit(solution)/shard_map/psum | solution.py:144
  181.7 4.3 collective-permute-start
  190.5 9.3 %fusion.29 = bf16[2,16,3,768]{3,1,2,0:T(8,128)(2,1)S(1)} fusion(bf16[1,3072,3,768]{1,3,2,0:T(8,128)(2,1)} %copy.75, bf16[2,16,3072]{2,1,0:T(8,128)(2,1)S(1)} %get-tuple-element.37, f32[2,16]{1,0:T(2,128)S(1)} %add_rsqrt_fusion.3, f32[2,16]{1,0:T(2,128)S(1)} %broadcast_multiply_fusion.3, f32[3072]{0:T(1024)S(1)} %get-tuple-element.76, ...), kind=kOutput, calls=%fused_computation.58 | convolution fusion | flops 453648384 | bytes 14524672 | tf_op jit(solution)/shard_map/dot_general | solution.py:103
  201.3 19.7 %all_gather.41 = bf16[2,128,2,768]{3,1,2,0:T(8,128)(2,1)S(1)} all-gather(bf16[2,8,2,768]{3,1,2,0:T(8,128)(2,1)S(1)} %get-tuple-element.71), channel_id=1, replica_groups=mesh['section'=2,'seq'=16,'mp'=4] {'seq'}, dimensions={1}, use_global_device_ids=true | all-gather | bytes 835584 | tf_op jit(solution)/shard_map/all_gather | solution.py:111
  222.3 19.1 %all_gather.40 = bf16[2,128,2,768]{3,1,2,0:T(8,128)(2,1)S(1)} all-gather(bf16[2,8,2,768]{3,1,2,0:T(8,128)(2,1)} %get-tuple-element.72), channel_id=1, replica_groups=mesh['section'=2,'seq'=16,'mp'=4] {'seq'}, dimensions={1}, use_global_device_ids=true | all-gather | bytes 835584 | tf_op jit(solution)/shard_map/all_gather | solution.py:110
  246.2 5.8 broadcast_in_dim.488
  264.9 47.4 %all-reduce.9.cloned.1.call-done = f32[2,16,3072]{2,1,0:T(8,128)} async-done(((f32[2,16,3072]{2,1,0:T(8,128)}), f32[2,16,3072]{2,1,0:T(8,128)}) %all-reduce.9.cloned.1.call-update) | async-done | bytes 393232 | tf_op jit(solution)/shard_map/psum | solution.py:144
  313.4 4.3 collective-permute-start.1
  322.2 9.3 %fusion.32 = bf16[2,16,3,768]{3,1,2,0:T(8,128)(2,1)S(1)} fusion(bf16[1,3072,3,768]{1,3,2,0:T(8,128)(2,1)} %copy.75, bf16[2,16,3072]{2,1,0:T(8,128)(2,1)S(1)} %get-tuple-element.32, f32[2,16]{1,0:T(2,128)S(1)} %add_rsqrt_fusion.2, f32[2,16]{1,0:T(2,128)S(1)} %broadcast_multiply_fusion.2, f32[3072]{0:T(1024)S(1)} %get-tuple-element.76, ...), kind=kOutput, calls=%fused_computation.59 | convolution fusion | flops 453648384 | bytes 14524672 | tf_op jit(solution)/shard_map/dot_general | solution.py:103
  333.6 19.7 %all_gather.43 = bf16[2,128,2,768]{3,1,2,0:T(8,128)(2,1)S(1)} all-gather(bf16[2,8,2,768]{3,1,2,0:T(8,128)(2,1)S(1)} %get-tuple-element.69), channel_id=1, replica_groups=mesh['section'=2,'seq'=16,'mp'=4] {'seq'}, dimensions={1}, use_global_device_ids=true | all-gather | bytes 835584 | tf_op jit(solution)/shard_map/all_gather | solution.py:111
  354.6 19.2 %all_gather.42 = bf16[2,128,2,768]{3,1,2,0:T(8,128)(2,1)S(1)} all-gather(bf16[2,8,2,768]{3,1,2,0:T(8,128)(2,1)} %get-tuple-element.70), channel_id=1, replica_groups=mesh['section'=2,'seq'=16,'mp'=4] {'seq'}, dimensions={1}, use_global_device_ids=true | all-gather | bytes 835584 | tf_op jit(solution)/shard_map/all_gather | solution.py:110
  378.5 5.7 broadcast_in_dim.495
  397.2 47.5 %all-reduce.11.cloned.1.call-done = f32[2,16,3072]{2,1,0:T(8,128)} async-done(((f32[2,16,3072]{2,1,0:T(8,128)}), f32[2,16,3072]{2,1,0:T(8,128)}) %all-reduce.11.cloned.1.call-update) | async-done | bytes 393232 | tf_op jit(solution)/shard_map/psum | solution.py:144
  454.6 9.3 %fusion.35 = bf16[2,16,3,768]{3,1,2,0:T(8,128)(2,1)S(1)} fusion(bf16[1,3072,3,768]{1,3,2,0:T(8,128)(2,1)} %copy.75, bf16[2,16,3072]{2,1,0:T(8,128)(2,1)S(1)} %get-tuple-element.27, f32[2,16]{1,0:T(2,128)S(1)} %add_rsqrt_fusion.1, f32[2,16]{1,0:T(2,128)S(1)} %broadcast_multiply_fusion.1, f32[3072]{0:T(1024)S(1)} %get-tuple-element.76, ...), kind=kOutput, calls=%fused_computation.60 | convolution fusion | flops 453648384 | bytes 14524672 | tf_op jit(solution)/shard_map/dot_general | solution.py:103
  465.4 19.7 %all_gather.45 = bf16[2,128,2,768]{3,1,2,0:T(8,128)(2,1)S(1)} all-gather(bf16[2,8,2,768]{3,1,2,0:T(8,128)(2,1)S(1)} %get-tuple-element.67), channel_id=1, replica_groups=mesh['section'=2,'seq'=16,'mp'=4] {'seq'}, dimensions={1}, use_global_device_ids=true | all-gather | bytes 835584 | tf_op jit(solution)/shard_map/all_gather | solution.py:111
  486.4 19.2 %all_gather.44 = bf16[2,128,2,768]{3,1,2,0:T(8,128)(2,1)S(1)} all-gather(bf16[2,8,2,768]{3,1,2,0:T(8,128)(2,1)} %get-tuple-element.68), channel_id=1, replica_groups=mesh['section'=2,'seq'=16,'mp'=4] {'seq'}, dimensions={1}, use_global_device_ids=true | all-gather | bytes 835584 | tf_op jit(solution)/shard_map/all_gather | solution.py:110
  510.4 5.8 broadcast_in_dim.502
  529.1 47.4 %all-reduce.13.cloned.1.call-done = f32[2,16,3072]{2,1,0:T(8,128)} async-done(((f32[2,16,3072]{2,1,0:T(8,128)}), f32[2,16,3072]{2,1,0:T(8,128)}) %all-reduce.13.cloned.1.call-update) | async-done | bytes 393232 | tf_op jit(solution)/shard_map/psum | solution.py:144
  586.4 9.3 %fusion.38 = bf16[2,16,3,768]{3,1,2,0:T(8,128)(2,1)S(1)} fusion(bf16[1,3072,3,768]{1,3,2,0:T(8,128)(2,1)} %copy.75, bf16[2,16,3072]{2,1,0:T(8,128)(2,1)S(1)} %get-tuple-element.22, f32[2,16]{1,0:T(2,128)S(1)} %add_rsqrt_fusion, f32[2,16]{1,0:T(2,128)S(1)} %broadcast_multiply_fusion, f32[3072]{0:T(1024)S(1)} %get-tuple-element.76, ...), kind=kOutput, calls=%fused_computation.61 | convolution fusion | flops 453648384 | bytes 14524672 | tf_op jit(solution)/shard_map/dot_general | solution.py:103
  597.4 19.7 %all_gather.47 = bf16[2,128,2,768]{3,1,2,0:T(8,128)(2,1)S(1)} all-gather(bf16[2,8,2,768]{3,1,2,0:T(8,128)(2,1)S(1)} %get-tuple-element.65), channel_id=1, replica_groups=mesh['section'=2,'seq'=16,'mp'=4] {'seq'}, dimensions={1}, use_global_device_ids=true | all-gather | bytes 835584 | tf_op jit(solution)/shard_map/all_gather | solution.py:111
  618.3 19.2 %all_gather.46 = bf16[2,128,2,768]{3,1,2,0:T(8,128)(2,1)S(1)} all-gather(bf16[2,8,2,768]{3,1,2,0:T(8,128)(2,1)} %get-tuple-element.66), channel_id=1, replica_groups=mesh['section'=2,'seq'=16,'mp'=4] {'seq'}, dimensions={1}, use_global_device_ids=true | all-gather | bytes 835584 | tf_op jit(solution)/shard_map/all_gather | solution.py:110
  640.4 5.7 broadcast_in_dim.509
  663.0 43.2 %all-reduce.15.cloned.1.call-done = f32[2,16,3072]{2,1,0:T(8,128)} async-done(((f32[2,16,3072]{2,1,0:T(8,128)}), f32[2,16,3072]{2,1,0:T(8,128)}) %all-reduce.15.cloned.1.call-update) | async-done | bytes 393232 | tf_op jit(solution)/shard_map/psum | solution.py:144
  (287 shorter events, 138.7 us)
Async XLA Ops:
  7.2 20.3 %copy-start = (bf16[1,512,2304]{2,1,0:T(8,128)(2,1)S(1)}, bf16[1,512,2304]{2,1,0:T(8,128)(2,1)}, u32[]{:S(2)}) copy-start(bf16[1,512,2304]{2,1,0:T(8,128)(2,1)} %param.14) | copy-start | bytes 7077892
  7.2 95.7 %all-gather.4.cloned.1.call-start = ((), (), s32[]{:S(2)}) async-start(), calls=%async_computation.5 | async-start | bytes 3342336 | tf_op jit(solution)/shard_map/all_gather | solution.py:83
  7.9 172.7 %all-reduce.7.cloned.1.call-start = ((), (), s32[]{:S(2)}) async-start(), calls=%async_computation | async-start | bytes 786432 | tf_op jit(solution)/shard_map/psum | solution.py:144
  8.0 26.3 %copy-start.34 = (bf16[2,4,8,3072]{3,2,1,0:T(8,128)(2,1)S(1)}, bf16[2,4,8,3072]{3,2,1,0:T(8,128)(2,1)}, u32[]{:S(2)}) copy-start(bf16[2,4,8,3072]{3,2,1,0:T(8,128)(2,1)} %param.9) | copy-start | bytes 1179652
  26.6 8.4 %copy-start.9 = (bf16[2,8,3072]{2,1,0:T(8,128)(2,1)S(1)}, bf16[2,8,3072]{2,1,0:T(8,128)(2,1)}, u32[]{:S(2)}) copy-start(bf16[2,8,3072]{2,1,0:T(8,128)(2,1)} %param.10) | copy-start | bytes 294916
  44.7 43.5 %copy-start.22 = (bf16[2,16,3,768]{3,1,2,0:T(8,128)(2,1)}, bf16[2,16,3,768]{3,1,2,0:T(8,128)(2,1)S(1)}, u32[]{:S(2)}) copy-start(bf16[2,16,3,768]{3,1,2,0:T(8,128)(2,1)S(1)} %fusion.26) | copy-start | bytes 442372
  44.9 56.1 %copy-start.18 = (bf16[2,16,12,64]{3,2,1,0:T(8,128)(2,1)}, bf16[2,16,12,64]{3,2,1,0:T(8,128)(2,1)S(1)}, u32[]{:S(2)}) copy-start(bf16[2,16,12,64]{3,2,1,0:T(8,128)(2,1)S(1)} %reshape_squeeze.63) | copy-start | bytes 147460
  131.0 59.1 %copy-start.40 = (bf16[2,8,3072]{2,1,0:T(8,128)(2,1)S(1)}, bf16[2,8,3072]{2,1,0:T(8,128)(2,1)}, u32[]{:S(2)}) copy-start(bf16[2,8,3072]{2,1,0:T(8,128)(2,1)} %get-tuple-element.57) | copy-start | bytes 294916
  135.1 177.3 %all-reduce.9.cloned.1.call-start = ((), (), s32[]{:S(2)}) async-start(), calls=%async_computation.1 | async-start | bytes 786432 | tf_op jit(solution)/shard_map/psum | solution.py:144
  135.2 55.0 %copy-start.46 = (pred[4]{0:T(512)(128)(4,1)}, pred[4]{0:T(512)(128)(4,1)S(1)}, u32[]{:S(2)}) copy-start(pred[4]{0:T(512)(128)(4,1)S(1)} %iota_compare_fusion.3) | copy-start | bytes 16
  181.7 8.8 %copy-start.26 = (bf16[2,16,3072]{2,1,0:T(8,128)(2,1)}, bf16[2,16,3072]{2,1,0:T(8,128)(2,1)S(1)}, u32[]{:S(2)}) copy-start(bf16[2,16,3072]{2,1,0:T(8,128)(2,1)S(1)} %fusion.136) | copy-start | bytes 589828
  181.7 8.4 %collective-permute-start = (bf16[2,16,3072]{2,1,0:T(8,128)(2,1)S(1)}, bf16[2,16,3072]{2,1,0:T(8,128)(2,1)S(1)}, u32[]{:S(2)}, u32[]{:S(2)}) collective-permute-start(bf16[2,16,3072]{2,1,0:T(8,128)(2,1)S(1)} %fusion.136), channel_id=1, source_target_pairs={{0,64},{1,65},{2,66},{3,67},{4,68},{5,69},{6,70},{7,71},{8,72},{9,... | collective-permute-start | bytes 589832 | tf_op jit(solution)/shard_map/ppermute | solution.py:15
  260.8 61.1 %copy-start.39 = (bf16[2,8,3072]{2,1,0:T(8,128)(2,1)S(1)}, bf16[2,8,3072]{2,1,0:T(8,128)(2,1)}, u32[]{:S(2)}) copy-start(bf16[2,8,3072]{2,1,0:T(8,128)(2,1)} %get-tuple-element.54) | copy-start | bytes 294916
  264.8 179.9 %all-reduce.11.cloned.1.call-start = ((), (), s32[]{:S(2)}) async-start(), calls=%async_computation.2 | async-start | bytes 786432 | tf_op jit(solution)/shard_map/psum | solution.py:144
  264.9 57.1 %copy-start.48 = (pred[4]{0:T(512)(128)(4,1)}, pred[4]{0:T(512)(128)(4,1)S(1)}, u32[]{:S(2)}) copy-start(pred[4]{0:T(512)(128)(4,1)S(1)} %iota_compare_fusion.2) | copy-start | bytes 16
  313.4 8.8 %copy-start.28 = (bf16[2,16,3072]{2,1,0:T(8,128)(2,1)}, bf16[2,16,3072]{2,1,0:T(8,128)(2,1)S(1)}, u32[]{:S(2)}) copy-start(bf16[2,16,3072]{2,1,0:T(8,128)(2,1)S(1)} %fusion.137) | copy-start | bytes 589828
  313.4 8.4 %collective-permute-start.1 = (bf16[2,16,3072]{2,1,0:T(8,128)(2,1)S(1)}, bf16[2,16,3072]{2,1,0:T(8,128)(2,1)S(1)}, u32[]{:S(2)}, u32[]{:S(2)}) collective-permute-start(bf16[2,16,3072]{2,1,0:T(8,128)(2,1)S(1)} %fusion.137), channel_id=1, source_target_pairs={{0,64},{1,65},{2,66},{3,67},{4,68},{5,69},{6,70},{7,71},{8,72},{9,... | collective-permute-start | bytes 589832 | tf_op jit(solution)/shard_map/ppermute | solution.py:15
  393.1 61.2 %copy-start.38 = (bf16[2,8,3072]{2,1,0:T(8,128)(2,1)S(1)}, bf16[2,8,3072]{2,1,0:T(8,128)(2,1)}, u32[]{:S(2)}) copy-start(bf16[2,8,3072]{2,1,0:T(8,128)(2,1)} %get-tuple-element.55) | copy-start | bytes 294916
  397.1 179.4 %all-reduce.13.cloned.1.call-start = ((), (), s32[]{:S(2)}) async-start(), calls=%async_computation.3 | async-start | bytes 786432 | tf_op jit(solution)/shard_map/psum | solution.py:144
  445.8 8.8 %copy-start.30 = (bf16[2,16,3072]{2,1,0:T(8,128)(2,1)}, bf16[2,16,3072]{2,1,0:T(8,128)(2,1)S(1)}, u32[]{:S(2)}) copy-start(bf16[2,16,3072]{2,1,0:T(8,128)(2,1)S(1)} %fusion.138) | copy-start | bytes 589828
  445.8 8.4 %collective-permute-start.2 = (bf16[2,16,3072]{2,1,0:T(8,128)(2,1)S(1)}, bf16[2,16,3072]{2,1,0:T(8,128)(2,1)S(1)}, u32[]{:S(2)}, u32[]{:S(2)}) collective-permute-start(bf16[2,16,3072]{2,1,0:T(8,128)(2,1)S(1)} %fusion.138), channel_id=1, source_target_pairs={{0,64},{1,65},{2,66},{3,67},{4,68},{5,69},{6,70},{7,71},{8,72},{9,... | collective-permute-start | bytes 589832 | tf_op jit(solution)/shard_map/ppermute | solution.py:15
  524.9 61.1 %copy-start.37 = (bf16[2,8,3072]{2,1,0:T(8,128)(2,1)S(1)}, bf16[2,8,3072]{2,1,0:T(8,128)(2,1)}, u32[]{:S(2)}) copy-start(bf16[2,8,3072]{2,1,0:T(8,128)(2,1)} %get-tuple-element.53) | copy-start | bytes 294916
  529.0 177.2 %all-reduce.15.cloned.1.call-start = ((), (), s32[]{:S(2)}) async-start(), calls=%async_computation.4 | async-start | bytes 786432 | tf_op jit(solution)/shard_map/psum | solution.py:144
  577.6 8.6 %copy-start.32 = (bf16[2,16,3072]{2,1,0:T(8,128)(2,1)}, bf16[2,16,3072]{2,1,0:T(8,128)(2,1)S(1)}, u32[]{:S(2)}) copy-start(bf16[2,16,3072]{2,1,0:T(8,128)(2,1)S(1)} %fusion.139) | copy-start | bytes 589828
  577.6 8.4 %collective-permute-start.3 = (bf16[2,16,3072]{2,1,0:T(8,128)(2,1)S(1)}, bf16[2,16,3072]{2,1,0:T(8,128)(2,1)S(1)}, u32[]{:S(2)}, u32[]{:S(2)}) collective-permute-start(bf16[2,16,3072]{2,1,0:T(8,128)(2,1)S(1)} %fusion.139), channel_id=1, source_target_pairs={{0,64},{1,65},{2,66},{3,67},{4,68},{5,69},{6,70},{7,71},{8,72},{9,... | collective-permute-start | bytes 589832 | tf_op jit(solution)/shard_map/ppermute | solution.py:15
  654.4 7.6 %copy-start.45 = (pred[4]{0:T(512)(128)(4,1)S(1)}, pred[4]{0:T(512)(128)(4,1)}, u32[]{:S(2)}) copy-start(pred[4]{0:T(512)(128)(4,1)} %copy-done.44) | copy-start | bytes 16
  654.4 7.6 %copy-start.47 = (pred[4]{0:T(512)(128)(4,1)S(1)}, pred[4]{0:T(512)(128)(4,1)}, u32[]{:S(2)}) copy-start(pred[4]{0:T(512)(128)(4,1)} %copy-done.46) | copy-start | bytes 16
  654.4 52.9 %copy-start.27 = (bf16[2,16,3072]{2,1,0:T(8,128)(2,1)S(1)}, bf16[2,16,3072]{2,1,0:T(8,128)(2,1)}, u32[]{:S(2)}) copy-start(bf16[2,16,3072]{2,1,0:T(8,128)(2,1)} %copy-done.26) | copy-start | bytes 589828
  654.4 52.9 %copy-start.29 = (bf16[2,16,3072]{2,1,0:T(8,128)(2,1)S(1)}, bf16[2,16,3072]{2,1,0:T(8,128)(2,1)}, u32[]{:S(2)}) copy-start(bf16[2,16,3072]{2,1,0:T(8,128)(2,1)} %copy-done.28) | copy-start | bytes 589828
  654.4 52.9 %copy-start.31 = (bf16[2,16,3072]{2,1,0:T(8,128)(2,1)S(1)}, bf16[2,16,3072]{2,1,0:T(8,128)(2,1)}, u32[]{:S(2)}) copy-start(bf16[2,16,3072]{2,1,0:T(8,128)(2,1)} %copy-done.30) | copy-start | bytes 589828
  654.4 52.9 %copy-start.33 = (bf16[2,16,3072]{2,1,0:T(8,128)(2,1)S(1)}, bf16[2,16,3072]{2,1,0:T(8,128)(2,1)}, u32[]{:S(2)}) copy-start(bf16[2,16,3072]{2,1,0:T(8,128)(2,1)} %copy-done.32) | copy-start | bytes 589828
  654.4 54.5 %copy-start.1 = (bf16[1,512,2304]{2,1,0:T(8,128)(2,1)S(1)}, bf16[1,512,2304]{2,1,0:T(8,128)(2,1)}, u32[]{:S(2)}) copy-start(bf16[1,512,2304]{2,1,0:T(8,128)(2,1)} %param.14) | copy-start | bytes 7077892
  (34 other events, 87.0 us)
Sparse Core Ops, SparseCore 0:
  10.2 52.0 all-gather.3
  135.2 45.3 all-reduce.6
  264.9 47.3 all-reduce.8
  397.3 47.4 all-reduce.10
  529.1 47.3 all-reduce.12
  658.8 47.4 all-reduce.14
where the time goes:
time: 723 us; the launch traced here: 716 us
  waiting for transfers between devices  246 us (34%)
  blocking collectives  203 us (28%)
  local copies, waits for them, and re-layouts  116 us (16%)
  matrix products  86.7 us (12%)
  other arithmetic  30.2 us (4%)
  starting transfers between devices  17.5 us (2%)
  between operations  16.3 us (2%)
    psum x5, waiting for transfers between devices, body(): summed = lax.psum(partial_out, 'mp')  231 us
    all_gather x5, blocking collectives, body(): lax.all_gather(key_value[:, per_dev:], 'seq', axis=1, tiled=True)  103 us
    all_gather x5, blocking collectives, body(): lax.all_gather(key_value[:, :per_dev], 'seq', axis=1, tiled=True)  94.4 us
    broadcast_in_dim x15, local copies, waits for them, and re-layouts, body(): jnp.where(current[None, :, None, None, None], gathered_video[:, None], fr...  47 us
    dot_general x5, matrix products, body(): jnp.dot(normed.reshape(-1, model_width), weight_qkv, preferred_element_ty...  46.6 us
    unnamed x117, local copies, waits for them, and re-layouts  41 us
    dot_general x5, matrix products, body(): jnp.dot(attended, weight_out, preferred_element_type=jnp.float32)  20.3 us
    ppermute x4, starting transfers between devices, passed_along(): lax.ppermute(value, axis, [(source, source + steps) for source in range(l...  17.3 us
  transfers between devices with their start and end apart: 10, of which 9 were waited for; matrix products, arithmetic and copies ran while one was open for 7% of the time, Pallas kernels for 0%

commit v1 on v0

--- a/solution.py
+++ b/solution.py
@@ -141,7 +141,7 @@
         partial_out = jnp.dot(attended, weight_out, preferred_element_type=jnp.float32).reshape(
             requests, row_count, model_width
         )
-        summed = lax.psum(partial_out, "mp")
+        summed = jnp.sum(lax.all_gather(partial_out, "mp"), 0)
         result = (token_rows.astype(jnp.float32) + gate_vec * summed).astype(jnp.bfloat16)
         out_video = jnp.where(current[None, :, None, None], result[:, None, :per_dev], out_video)
         out_text = jnp.where(patch_now == 0, result[:, per_dev:], out_text)

time: 723 us -> 665 us (0.920)
  waiting for transfers between devices: 246 us -> 189 us
    psum x5 -> x0, waiting for transfers between devices: 231 us -> none  [body(): summed = lax.psum(partial_out, 'mp')]
    all_gather x0 -> x5, waiting for transfers between devices: none -> 172 us  [body(): summed = jnp.sum(lax.all_gather(partial_out, 'mp'), 0)]
    reduce_sum x0 -> x5, other arithmetic: none -> 7.81 us  [body(): summed = jnp.sum(lax.all_gather(partial_out, 'mp'), 0)]
    unnamed x117 -> x145, local copies, waits for them, and re-layouts: 41 us -> 41.5 us
where the time goes in v1:
time: 665 us; the launch traced here: 658 us
  blocking collectives  203 us (31%)
  waiting for transfers between devices  189 us (28%)
  local copies, waits for them, and re-layouts  110 us (17%)
  matrix products  86.4 us (13%)
  other arithmetic  35.2 us (5%)
  starting transfers between devices  17.5 us (3%)
  between operations  16.3 us (2%)
    all_gather x5, waiting for transfers between devices, body(): summed = jnp.sum(lax.all_gather(partial_out, 'mp'), 0)  172 us
    all_gather x5, blocking collectives, body(): lax.all_gather(key_value[:, per_dev:], 'seq', axis=1, tiled=True)  103 us
    all_gather x5, blocking collectives, body(): lax.all_gather(key_value[:, :per_dev], 'seq', axis=1, tiled=True)  94.2 us
    dot_general x5, matrix products, body(): jnp.dot(normed.reshape(-1, model_width), weight_qkv, preferred_element_ty...  46.6 us
    broadcast_in_dim x15, local copies, waits for them, and re-layouts, body(): jnp.where(current[None, :, None, None, None], gathered_video[:, None], fr...  44.7 us
    unnamed x145, local copies, waits for them, and re-layouts  41.5 us
    dot_general x5, matrix products, body(): jnp.dot(attended, weight_out, preferred_element_type=jnp.float32)  20.1 us
    ppermute x4, starting transfers between devices, passed_along(): lax.ppermute(value, axis, [(source, source + steps) for source in range(l...  17.3 us
  transfers between devices with their start and end apart: 10, of which 9 were waited for; matrix products, arithmetic and copies ran while one was open for 7% of the time, Pallas kernels for 0%

profile of v1, /device:TPU:1, one launch (start us, length us, event | category | flops | bytes accessed | tf_op | source)
XLA Modules:
  0.0 658.0 jit_solution(17361726341779367216)
XLA Ops:
  8.0 18.7 %copy.75 = bf16[1,3072,3,768]{1,3,2,0:T(8,128)(2,1)} copy(bf16[1,3072,3,768]{3,1,2,0:T(8,128)(2,1)} %param.15) | data formatting | bytes 28311552 | tf_op args[6]
  27.9 6.4 all-gather.6
  35.4 9.3 %fusion.26 = bf16[2,16,3,768]{3,1,2,0:T(8,128)(2,1)S(1)} fusion(bf16[1,3072,3,768]{1,3,2,0:T(8,128)(2,1)} %copy.75, f32[3072]{0:T(1024)S(1)} %get-tuple-element.76, f32[3072]{0:T(1024)S(1)} %get-tuple-element.77, f32[2,16]{1,0:T(2,128)S(1)} %add_rsqrt_fusion.4, f32[2,16]{1,0:T(2,128)S(1)} %broadcast_multiply_fusion.4, ...), kind=kOutput, calls=%fused_computation.57 | convolution fusion | flops 454139904 | bytes 14524673 | tf_op jit(solution)/shard_map/dot_general | solution.py:103
  44.9 23.9 %all_gather.53 = bf16[2,128,2,768]{3,1,2,0:T(8,128)(2,1)S(1)} all-gather(bf16[2,8,2,768]{3,1,2,0:T(8,128)(2,1)S(1)} %get-tuple-element.73), channel_id=1, replica_groups=mesh['section'=2,'seq'=16,'mp'=4] {'seq'}, dimensions={1}, use_global_device_ids=true | all-gather | bytes 835584 | tf_op jit(solution)/shard_map/all_gather | solution.py:111
  70.1 17.4 %all_gather.52 = bf16[2,128,2,768]{3,1,2,0:T(8,128)(2,1)S(1)} all-gather(bf16[2,8,2,768]{3,1,2,0:T(8,128)(2,1)S(1)} %get-tuple-element.74), channel_id=1, replica_groups=mesh['section'=2,'seq'=16,'mp'=4] {'seq'}, dimensions={1}, use_global_device_ids=true | all-gather | bytes 835584 | tf_op jit(solution)/shard_map/all_gather | solution.py:110
  90.4 5.7 broadcast_in_dim.475
  103.1 9.4 %fusion.259 = (bf16[2,512,1,768]{3,2,1,0:T(2,128)(2,1)}, bf16[2,512,1,768]{3,2,1,0:T(2,128)(2,1)}) fusion(bf16[2,512,2,768]{3,2,1,0:T(2,128)(2,1)} %bitcast.358), kind=kLoop, calls=%fused_computation.383 | loop fusion | bytes 6291456 | tf_op jit(solution)/shard_map/slice | solution.py:36
  112.5 6.8 %copy.115 = bf16[2,512,1,768]{1,3,0,2:T(8,128)(2,1)S(1)} copy(bf16[2,512,1,768]{3,2,1,0:T(2,128)(2,1)} %get-tuple-element.52) | data formatting | bytes 3145728
  119.3 8.2 %copy.114 = bf16[2,512,1,768]{1,3,0,2:T(8,128)(2,1)} copy(bf16[2,512,1,768]{3,2,1,0:T(2,128)(2,1)} %get-tuple-element.51) | data formatting | bytes 3145728
  136.3 33.3 %all-gather.16.cloned.1.call-done = f32[8,16,3072]{2,1,0:T(8,128)} async-done(((f32[2,16,3072]{2,1,0:T(8,128)}), f32[8,16,3072]{2,1,0:T(8,128)}) %all-gather.16.cloned.1.call-update) | async-done | bytes 1572880 | tf_op jit(solution)/shard_map/all_gather | solution.py:144
  171.2 4.3 collective-permute-start
  180.0 9.3 %fusion.29 = bf16[2,16,3,768]{3,1,2,0:T(8,128)(2,1)S(1)} fusion(bf16[1,3072,3,768]{1,3,2,0:T(8,128)(2,1)} %copy.75, bf16[2,16,3072]{2,1,0:T(8,128)(2,1)S(1)} %get-tuple-element.37, f32[2,16]{1,0:T(2,128)S(1)} %add_rsqrt_fusion.3, f32[2,16]{1,0:T(2,128)S(1)} %broadcast_multiply_fusion.3, f32[3072]{0:T(1024)S(1)} %get-tuple-element.76, ...), kind=kOutput, calls=%fused_computation.58 | convolution fusion | flops 453648384 | bytes 14524672 | tf_op jit(solution)/shard_map/dot_general | solution.py:103
  190.2 19.7 %all_gather.57 = bf16[2,128,2,768]{3,1,2,0:T(8,128)(2,1)S(1)} all-gather(bf16[2,8,2,768]{3,1,2,0:T(8,128)(2,1)S(1)} %get-tuple-element.71), channel_id=1, replica_groups=mesh['section'=2,'seq'=16,'mp'=4] {'seq'}, dimensions={1}, use_global_device_ids=true | all-gather | bytes 835584 | tf_op jit(solution)/shard_map/all_gather | solution.py:111
  211.2 19.2 %all_gather.56 = bf16[2,128,2,768]{3,1,2,0:T(8,128)(2,1)S(1)} all-gather(bf16[2,8,2,768]{3,1,2,0:T(8,128)(2,1)S(1)} %get-tuple-element.72), channel_id=1, replica_groups=mesh['section'=2,'seq'=16,'mp'=4] {'seq'}, dimensions={1}, use_global_device_ids=true | all-gather | bytes 835584 | tf_op jit(solution)/shard_map/all_gather | solution.py:110
  235.2 5.7 broadcast_in_dim.488
  253.8 35.2 %all-gather.18.cloned.1.call-done = f32[8,16,3072]{2,1,0:T(8,128)} async-done(((f32[2,16,3072]{2,1,0:T(8,128)}), f32[8,16,3072]{2,1,0:T(8,128)}) %all-gather.18.cloned.1.call-update) | async-done | bytes 1572880 | tf_op jit(solution)/shard_map/all_gather | solution.py:144
  290.6 4.3 collective-permute-start.1
  299.4 9.3 %fusion.32 = bf16[2,16,3,768]{3,1,2,0:T(8,128)(2,1)S(1)} fusion(bf16[1,3072,3,768]{1,3,2,0:T(8,128)(2,1)} %copy.75, bf16[2,16,3072]{2,1,0:T(8,128)(2,1)S(1)} %get-tuple-element.32, f32[2,16]{1,0:T(2,128)S(1)} %add_rsqrt_fusion.2, f32[2,16]{1,0:T(2,128)S(1)} %broadcast_multiply_fusion.2, f32[3072]{0:T(1024)S(1)} %get-tuple-element.76, ...), kind=kOutput, calls=%fused_computation.59 | convolution fusion | flops 453648384 | bytes 14524672 | tf_op jit(solution)/shard_map/dot_general | solution.py:103
  310.2 19.7 %all_gather.60 = bf16[2,128,2,768]{3,1,2,0:T(8,128)(2,1)S(1)} all-gather(bf16[2,8,2,768]{3,1,2,0:T(8,128)(2,1)S(1)} %get-tuple-element.69), channel_id=1, replica_groups=mesh['section'=2,'seq'=16,'mp'=4] {'seq'}, dimensions={1}, use_global_device_ids=true | all-gather | bytes 835584 | tf_op jit(solution)/shard_map/all_gather | solution.py:111
  331.2 19.4 %all_gather.59 = bf16[2,128,2,768]{3,1,2,0:T(8,128)(2,1)S(1)} all-gather(bf16[2,8,2,768]{3,1,2,0:T(8,128)(2,1)S(1)} %get-tuple-element.70), channel_id=1, replica_groups=mesh['section'=2,'seq'=16,'mp'=4] {'seq'}, dimensions={1}, use_global_device_ids=true | all-gather | bytes 835584 | tf_op jit(solution)/shard_map/all_gather | solution.py:110
  355.3 5.7 broadcast_in_dim.495
  374.0 35.2 %all-gather.20.cloned.1.call-done = f32[8,16,3072]{2,1,0:T(8,128)} async-done(((f32[2,16,3072]{2,1,0:T(8,128)}), f32[8,16,3072]{2,1,0:T(8,128)}) %all-gather.20.cloned.1.call-update) | async-done | bytes 1572880 | tf_op jit(solution)/shard_map/all_gather | solution.py:144
  419.6 9.3 %fusion.35 = bf16[2,16,3,768]{3,1,2,0:T(8,128)(2,1)S(1)} fusion(bf16[1,3072,3,768]{1,3,2,0:T(8,128)(2,1)} %copy.75, bf16[2,16,3072]{2,1,0:T(8,128)(2,1)S(1)} %get-tuple-element.27, f32[2,16]{1,0:T(2,128)S(1)} %add_rsqrt_fusion.1, f32[2,16]{1,0:T(2,128)S(1)} %broadcast_multiply_fusion.1, f32[3072]{0:T(1024)S(1)} %get-tuple-element.76, ...), kind=kOutput, calls=%fused_computation.60 | convolution fusion | flops 453648384 | bytes 14524672 | tf_op jit(solution)/shard_map/dot_general | solution.py:103
  429.8 19.7 %all_gather.63 = bf16[2,128,2,768]{3,1,2,0:T(8,128)(2,1)S(1)} all-gather(bf16[2,8,2,768]{3,1,2,0:T(8,128)(2,1)S(1)} %get-tuple-element.67), channel_id=1, replica_groups=mesh['section'=2,'seq'=16,'mp'=4] {'seq'}, dimensions={1}, use_global_device_ids=true | all-gather | bytes 835584 | tf_op jit(solution)/shard_map/all_gather | solution.py:111
  450.8 19.1 %all_gather.62 = bf16[2,128,2,768]{3,1,2,0:T(8,128)(2,1)S(1)} all-gather(bf16[2,8,2,768]{3,1,2,0:T(8,128)(2,1)S(1)} %get-tuple-element.68), channel_id=1, replica_groups=mesh['section'=2,'seq'=16,'mp'=4] {'seq'}, dimensions={1}, use_global_device_ids=true | all-gather | bytes 835584 | tf_op jit(solution)/shard_map/all_gather | solution.py:110
  474.7 5.8 broadcast_in_dim.502
  493.3 35.2 %all-gather.22.cloned.1.call-done = f32[8,16,3072]{2,1,0:T(8,128)} async-done(((f32[2,16,3072]{2,1,0:T(8,128)}), f32[8,16,3072]{2,1,0:T(8,128)}) %all-gather.22.cloned.1.call-update) | async-done | bytes 1572880 | tf_op jit(solution)/shard_map/all_gather | solution.py:144
  538.9 9.3 %fusion.38 = bf16[2,16,3,768]{3,1,2,0:T(8,128)(2,1)S(1)} fusion(bf16[1,3072,3,768]{1,3,2,0:T(8,128)(2,1)} %copy.75, bf16[2,16,3072]{2,1,0:T(8,128)(2,1)S(1)} %get-tuple-element.22, f32[2,16]{1,0:T(2,128)S(1)} %add_rsqrt_fusion, f32[2,16]{1,0:T(2,128)S(1)} %broadcast_multiply_fusion, f32[3072]{0:T(1024)S(1)} %get-tuple-element.76, ...), kind=kOutput, calls=%fused_computation.61 | convolution fusion | flops 453648384 | bytes 14524672 | tf_op jit(solution)/shard_map/dot_general | solution.py:103
  549.9 19.7 %all_gather.66 = bf16[2,128,2,768]{3,1,2,0:T(8,128)(2,1)S(1)} all-gather(bf16[2,8,2,768]{3,1,2,0:T(8,128)(2,1)S(1)} %get-tuple-element.65), channel_id=1, replica_groups=mesh['section'=2,'seq'=16,'mp'=4] {'seq'}, dimensions={1}, use_global_device_ids=true | all-gather | bytes 835584 | tf_op jit(solution)/shard_map/all_gather | solution.py:111
  570.9 19.2 %all_gather.65 = bf16[2,128,2,768]{3,1,2,0:T(8,128)(2,1)S(1)} all-gather(bf16[2,8,2,768]{3,1,2,0:T(8,128)(2,1)S(1)} %get-tuple-element.66), channel_id=1, replica_groups=mesh['section'=2,'seq'=16,'mp'=4] {'seq'}, dimensions={1}, use_global_device_ids=true | all-gather | bytes 835584 | tf_op jit(solution)/shard_map/all_gather | solution.py:110
  592.9 5.7 broadcast_in_dim.509
  612.7 33.2 %all-gather.24.cloned.1.call-done = f32[8,16,3072]{2,1,0:T(8,128)} async-done(((f32[2,16,3072]{2,1,0:T(8,128)}), f32[8,16,3072]{2,1,0:T(8,128)}) %all-gather.24.cloned.1.call-update) | async-done | bytes 1572880 | tf_op jit(solution)/shard_map/all_gather | solution.py:144
  (320 shorter events, 139.5 us)
Async XLA Ops:
  7.2 20.3 %copy-start = (bf16[1,512,2304]{2,1,0:T(8,128)(2,1)S(1)}, bf16[1,512,2304]{2,1,0:T(8,128)(2,1)}, u32[]{:S(2)}) copy-start(bf16[1,512,2304]{2,1,0:T(8,128)(2,1)} %param.14) | copy-start | bytes 7077892
  7.2 95.9 %all-gather.14.cloned.1.call-start = ((), (), s32[]{:S(2)}) async-start(), calls=%async_computation | async-start | bytes 3342336 | tf_op jit(solution)/shard_map/all_gather | solution.py:83
  7.9 161.6 %all-gather.16.cloned.1.call-start = ((), (), s32[]{:S(2)}) async-start(), calls=%async_computation.1 | async-start | bytes 1966080 | tf_op jit(solution)/shard_map/all_gather | solution.py:144
  44.7 42.8 %copy-start.22 = (bf16[2,16,3,768]{3,1,2,0:T(8,128)(2,1)}, bf16[2,16,3,768]{3,1,2,0:T(8,128)(2,1)S(1)}, u32[]{:S(2)}) copy-start(bf16[2,16,3,768]{3,1,2,0:T(8,128)(2,1)S(1)} %fusion.26) | copy-start | bytes 442372
  44.9 55.8 %copy-start.18 = (bf16[2,16,12,64]{3,2,1,0:T(8,128)(2,1)}, bf16[2,16,12,64]{3,2,1,0:T(8,128)(2,1)S(1)}, u32[]{:S(2)}) copy-start(bf16[2,16,12,64]{3,2,1,0:T(8,128)(2,1)S(1)} %reshape_squeeze.63) | copy-start | bytes 147460
  44.9 42.6 %copy-start.34 = (bf16[2,8,2,768]{3,1,2,0:T(8,128)(2,1)}, bf16[2,8,2,768]{3,1,2,0:T(8,128)(2,1)S(1)}, u32[]{:S(2)}) copy-start(bf16[2,8,2,768]{3,1,2,0:T(8,128)(2,1)S(1)} %get-tuple-element.74) | copy-start | bytes 147460
  136.2 43.4 %copy-start.47 = (bf16[2,8,3072]{2,1,0:T(8,128)(2,1)S(1)}, bf16[2,8,3072]{2,1,0:T(8,128)(2,1)}, u32[]{:S(2)}) copy-start(bf16[2,8,3072]{2,1,0:T(8,128)(2,1)} %get-tuple-element.57) | copy-start | bytes 294916
  136.2 152.8 %all-gather.18.cloned.1.call-start = ((), (), s32[]{:S(2)}) async-start(), calls=%async_computation.2 | async-start | bytes 1966080 | tf_op jit(solution)/shard_map/all_gather | solution.py:144
  136.3 43.4 %copy-start.60 = (pred[4]{0:T(512)(128)(4,1)}, pred[4]{0:T(512)(128)(4,1)S(1)}, u32[]{:S(2)}) copy-start(pred[4]{0:T(512)(128)(4,1)S(1)} %iota_compare_fusion.3) | copy-start | bytes 16
  171.2 18.1 %copy-start.26 = (bf16[2,16,3072]{2,1,0:T(8,128)(2,1)}, bf16[2,16,3072]{2,1,0:T(8,128)(2,1)S(1)}, u32[]{:S(2)}) copy-start(bf16[2,16,3072]{2,1,0:T(8,128)(2,1)S(1)} %fusion.136) | copy-start | bytes 589828
  171.2 8.4 %collective-permute-start = (bf16[2,16,3072]{2,1,0:T(8,128)(2,1)S(1)}, bf16[2,16,3072]{2,1,0:T(8,128)(2,1)S(1)}, u32[]{:S(2)}, u32[]{:S(2)}) collective-permute-start(bf16[2,16,3072]{2,1,0:T(8,128)(2,1)S(1)} %fusion.136), channel_id=1, source_target_pairs={{0,64},{1,65},{2,66},{3,67},{4,68},{5,69},{6,70},{7,71},{8,72},{9,... | collective-permute-start | bytes 589832 | tf_op jit(solution)/shard_map/ppermute | solution.py:15
  189.4 21.8 %copy-start.36 = (bf16[2,8,2,768]{3,1,2,0:T(8,128)(2,1)}, bf16[2,8,2,768]{3,1,2,0:T(8,128)(2,1)S(1)}, u32[]{:S(2)}) copy-start(bf16[2,8,2,768]{3,1,2,0:T(8,128)(2,1)S(1)} %get-tuple-element.72) | copy-start | bytes 147460
  253.7 45.3 %copy-start.46 = (bf16[2,8,3072]{2,1,0:T(8,128)(2,1)S(1)}, bf16[2,8,3072]{2,1,0:T(8,128)(2,1)}, u32[]{:S(2)}) copy-start(bf16[2,8,3072]{2,1,0:T(8,128)(2,1)} %get-tuple-element.54) | copy-start | bytes 294916
  253.7 155.5 %all-gather.20.cloned.1.call-start = ((), (), s32[]{:S(2)}) async-start(), calls=%async_computation.3 | async-start | bytes 1966080 | tf_op jit(solution)/shard_map/all_gather | solution.py:144
  253.8 45.4 %copy-start.62 = (pred[4]{0:T(512)(128)(4,1)}, pred[4]{0:T(512)(128)(4,1)S(1)}, u32[]{:S(2)}) copy-start(pred[4]{0:T(512)(128)(4,1)S(1)} %iota_compare_fusion.2) | copy-start | bytes 16
  290.6 18.1 %copy-start.28 = (bf16[2,16,3072]{2,1,0:T(8,128)(2,1)}, bf16[2,16,3072]{2,1,0:T(8,128)(2,1)S(1)}, u32[]{:S(2)}) copy-start(bf16[2,16,3072]{2,1,0:T(8,128)(2,1)S(1)} %fusion.137) | copy-start | bytes 589828
  290.6 8.4 %collective-permute-start.1 = (bf16[2,16,3072]{2,1,0:T(8,128)(2,1)S(1)}, bf16[2,16,3072]{2,1,0:T(8,128)(2,1)S(1)}, u32[]{:S(2)}, u32[]{:S(2)}) collective-permute-start(bf16[2,16,3072]{2,1,0:T(8,128)(2,1)S(1)} %fusion.137), channel_id=1, source_target_pairs={{0,64},{1,65},{2,66},{3,67},{4,68},{5,69},{6,70},{7,71},{8,72},{9,... | collective-permute-start | bytes 589832 | tf_op jit(solution)/shard_map/ppermute | solution.py:15
  309.4 21.8 %copy-start.38 = (bf16[2,8,2,768]{3,1,2,0:T(8,128)(2,1)}, bf16[2,8,2,768]{3,1,2,0:T(8,128)(2,1)S(1)}, u32[]{:S(2)}) copy-start(bf16[2,8,2,768]{3,1,2,0:T(8,128)(2,1)S(1)} %get-tuple-element.70) | copy-start | bytes 147460
  373.9 45.3 %copy-start.45 = (bf16[2,8,3072]{2,1,0:T(8,128)(2,1)S(1)}, bf16[2,8,3072]{2,1,0:T(8,128)(2,1)}, u32[]{:S(2)}) copy-start(bf16[2,8,3072]{2,1,0:T(8,128)(2,1)} %get-tuple-element.55) | copy-start | bytes 294916
  373.9 154.6 %all-gather.22.cloned.1.call-start = ((), (), s32[]{:S(2)}) async-start(), calls=%async_computation.4 | async-start | bytes 1966080 | tf_op jit(solution)/shard_map/all_gather | solution.py:144
  374.0 45.3 %copy-start.64 = (pred[4]{0:T(512)(128)(4,1)}, pred[4]{0:T(512)(128)(4,1)S(1)}, u32[]{:S(2)}) copy-start(pred[4]{0:T(512)(128)(4,1)S(1)} %iota_compare_fusion.1) | copy-start | bytes 16
  410.8 8.4 %collective-permute-start.2 = (bf16[2,16,3072]{2,1,0:T(8,128)(2,1)S(1)}, bf16[2,16,3072]{2,1,0:T(8,128)(2,1)S(1)}, u32[]{:S(2)}, u32[]{:S(2)}) collective-permute-start(bf16[2,16,3072]{2,1,0:T(8,128)(2,1)S(1)} %fusion.138), channel_id=1, source_target_pairs={{0,64},{1,65},{2,66},{3,67},{4,68},{5,69},{6,70},{7,71},{8,72},{9,... | collective-permute-start | bytes 589832 | tf_op jit(solution)/shard_map/ppermute | solution.py:15
  429.0 21.9 %copy-start.40 = (bf16[2,8,2,768]{3,1,2,0:T(8,128)(2,1)}, bf16[2,8,2,768]{3,1,2,0:T(8,128)(2,1)S(1)}, u32[]{:S(2)}) copy-start(bf16[2,8,2,768]{3,1,2,0:T(8,128)(2,1)S(1)} %get-tuple-element.68) | copy-start | bytes 147460
  493.2 45.3 %copy-start.44 = (bf16[2,8,3072]{2,1,0:T(8,128)(2,1)S(1)}, bf16[2,8,3072]{2,1,0:T(8,128)(2,1)}, u32[]{:S(2)}) copy-start(bf16[2,8,3072]{2,1,0:T(8,128)(2,1)} %get-tuple-element.53) | copy-start | bytes 294916
  493.3 152.7 %all-gather.24.cloned.1.call-start = ((), (), s32[]{:S(2)}) async-start(), calls=%async_computation.5 | async-start | bytes 1966080 | tf_op jit(solution)/shard_map/all_gather | solution.py:144
  493.3 45.2 %copy-start.66 = (pred[4]{0:T(512)(128)(4,1)}, pred[4]{0:T(512)(128)(4,1)S(1)}, u32[]{:S(2)}) copy-start(pred[4]{0:T(512)(128)(4,1)S(1)} %iota_compare_fusion.5) | copy-start | bytes 16
  530.1 18.1 %copy-start.32 = (bf16[2,16,3072]{2,1,0:T(8,128)(2,1)}, bf16[2,16,3072]{2,1,0:T(8,128)(2,1)S(1)}, u32[]{:S(2)}) copy-start(bf16[2,16,3072]{2,1,0:T(8,128)(2,1)S(1)} %fusion.139) | copy-start | bytes 589828
  530.1 8.4 %collective-permute-start.3 = (bf16[2,16,3072]{2,1,0:T(8,128)(2,1)S(1)}, bf16[2,16,3072]{2,1,0:T(8,128)(2,1)S(1)}, u32[]{:S(2)}, u32[]{:S(2)}) collective-permute-start(bf16[2,16,3072]{2,1,0:T(8,128)(2,1)S(1)} %fusion.139), channel_id=1, source_target_pairs={{0,64},{1,65},{2,66},{3,67},{4,68},{5,69},{6,70},{7,71},{8,72},{9,... | collective-permute-start | bytes 589832 | tf_op jit(solution)/shard_map/ppermute | solution.py:15
  549.9 21.0 %copy-start.42 = (bf16[2,8,2,768]{3,1,2,0:T(8,128)(2,1)}, bf16[2,8,2,768]{3,1,2,0:T(8,128)(2,1)S(1)}, u32[]{:S(2)}) copy-start(bf16[2,8,2,768]{3,1,2,0:T(8,128)(2,1)S(1)} %get-tuple-element.66) | copy-start | bytes 147460
  610.6 37.0 %copy-start.27 = (bf16[2,16,3072]{2,1,0:T(8,128)(2,1)S(1)}, bf16[2,16,3072]{2,1,0:T(8,128)(2,1)}, u32[]{:S(2)}) copy-start(bf16[2,16,3072]{2,1,0:T(8,128)(2,1)} %copy-done.26) | copy-start | bytes 589828
  610.6 37.0 %copy-start.29 = (bf16[2,16,3072]{2,1,0:T(8,128)(2,1)S(1)}, bf16[2,16,3072]{2,1,0:T(8,128)(2,1)}, u32[]{:S(2)}) copy-start(bf16[2,16,3072]{2,1,0:T(8,128)(2,1)} %copy-done.28) | copy-start | bytes 589828
  610.6 37.1 %copy-start.31 = (bf16[2,16,3072]{2,1,0:T(8,128)(2,1)S(1)}, bf16[2,16,3072]{2,1,0:T(8,128)(2,1)}, u32[]{:S(2)}) copy-start(bf16[2,16,3072]{2,1,0:T(8,128)(2,1)} %copy-done.30) | copy-start | bytes 589828
  (48 other events, 170.8 us)
Sparse Core Ops, SparseCore 0:
  10.2 52.0 all-gather.13
  136.4 33.1 all-gather.15
  253.8 35.0 all-gather.17
  374.0 35.0 all-gather.19
  493.4 35.0 all-gather.21
  610.8 35.0 all-gather.23
